TPU v7x, 32 devices: a whole 2x2x4 slice. The times are simulated.
32 devices in a mesh: parts: 2 (over x), rows: 16 (over z, y, core).
Axes of the slice: x: 2, y: 2, z: 4, core: 2. Of those that a mesh axis runs over, the one named last changes fastest.
Arguments:
- estimate: float32 [256, 2048], P(('parts', 'rows')), parts along dimension 0, may hold values from -6 to 6
- observed: float32 [256, 2048], P('parts', 'rows'), parts along dimension 0, may hold values from -6 to 6
- cotangent: float32 [256, 2048], P(('parts', 'rows')), parts along dimension 0
- zone_map: int32 [2, 16], P('parts'), parts along dimension 0, may hold values from 0 to 7
- bank_pick: int32 [2, 8], replicated, may hold values from 0 to 7
- psf_bank: float32 [8, 25], replicated, may hold values from 0.01 to 1
- w_first: bfloat16 [32, 1, 3, 3], replicated, may hold values from -2 to 2
- w_mid: bfloat16 [32, 32, 3, 3], replicated, may hold values from -0.375 to 0.375
- w_last: bfloat16 [1, 32, 3, 3], replicated, may hold values from -0.375 to 0.375
Outputs:
- denoised: float32 [256, 2048], P(('parts', 'rows')), parts along dimension 0
- grad_estimate: float32 [256, 2048], P(('parts', 'rows')), parts along dimension 0
- grad_first: float32 [64, 1, 3, 3], P('parts'), parts along dimension 0
- grad_mid: float32 [64, 32, 3, 3], P('parts'), parts along dimension 0
- grad_last: float32 [2, 32, 3, 3], P('parts'), parts along dimension 0
There are 2 independent parts, one for each index of `parts`. A program takes and returns all parts, laid end to end along the dimension named above; an argument that names none is the same for every part. Nothing has to cross between parts.
All inputs are finite; a program needn't handle non-finite values.
Results may differ from a plain program's by a relative error of at most 0.0071.
Values may be sent and summed in bfloat16 or wider, within the bound.
A program may use at most 256 MiB of HBM per device.

v0:
```python
import math
import jax
import jax.numpy as jnp
from jax import lax
from jax.sharding import PartitionSpec as P

BLK = 128
RAD = 12
STEP_SIZE = 2.0
GRAD_FACTOR = 8.0


def padded_2(shard, sides, width):
    for axis, dim in sides:
        size, length = (lax.axis_size(axis), shard.shape[dim])
        up = [(i, (i + 1) % size) for i in range(size - 1)]
        down = [(j, i) for i, j in up]
        last = lax.slice_in_dim(shard, length - width, length, axis=dim)
        leading = lax.slice_in_dim(shard, 0, width, axis=dim)
        before = lax.ppermute(last, axis, up)
        after = lax.ppermute(leading, axis, down)
        shard = jnp.concatenate([before, shard, after], axis=dim)
    return shard


def silu_slope(values):
    sigmoid = jax.nn.sigmoid(values)
    return sigmoid * (1.0 + values * (1.0 - sigmoid))


def flipped(weight):
    return jnp.transpose(jnp.flip(weight, (2, 3)), (1, 0, 2, 3))


def conv_rim(padded, weight):
    padding = ((0, 0), (1, 1))
    result = lax.conv_general_dilated(
        padded[None],
        weight,
        (1, 1),
        padding,
        dimension_numbers=("NCHW", "OIHW", "NCHW"),
        preferred_element_type=jnp.float32,
    )
    return result[0]


def weight_taps(framed, errors):
    height_cells = errors.shape[1]
    width_cells = errors.shape[2]
    all_taps = []
    for tap_row in range(3):
        line_taps = []
        for tap_col in range(3):
            window = framed[:, tap_row : tap_row + height_cells, tap_col : tap_col + width_cells]
            line_taps.append(
                jnp.einsum("ohw,chw->oc", errors, window, preferred_element_type=jnp.float32)
            )
        all_taps.append(jnp.stack(line_taps, axis=-1))
    return jnp.stack(all_taps, axis=-2)


def weight_grad(padded, errors, rim_dim):
    widths = [(0, 0), (0, 0), (0, 0)]
    widths[3 - rim_dim] = (1, 1)
    framed = jnp.pad(padded, widths)
    return weight_taps(framed, errors)


def blur_line(values, tap_coef, along, adjoint):
    length = values.shape[along]
    widths = [(0, 0), (0, 0)]
    widths[along] = (RAD, RAD)
    summed = jnp.zeros_like(values)
    padded = jnp.pad(values, widths)
    for offset in range(2 * RAD + 1):
        factor = tap_coef[offset][None, :] if along == 1 else tap_coef[offset][:, None]
        if adjoint:
            spread = jnp.pad(factor * values, widths)
            summed = summed + lax.slice_in_dim(
                spread, 2 * RAD - offset, 2 * RAD - offset + length, axis=along
            )
        else:
            summed = summed + factor * lax.slice_in_dim(padded, offset, offset + length, axis=along)
    return summed


def zone_kernels(psf_bank, bank_pick):
    norm_bank = psf_bank / jnp.sum(psf_bank, axis=1, keepdims=True)
    select = (
        bank_pick[:, :, None] == jnp.arange(psf_bank.shape[0], dtype=jnp.int32)[None, None, :]
    ).astype(jnp.float32)
    return jnp.einsum("rzb,bt->rzt", select, norm_bank, precision=lax.Precision.HIGHEST)


def tap_table(zone_line, kernel_table):
    zone_count = kernel_table.shape[0]
    onehot = (zone_line[:, None] == jnp.arange(zone_count, dtype=jnp.int32)[None, :]).astype(
        jnp.float32
    )
    per_block = jnp.einsum("nz,zt->tn", onehot, kernel_table, precision=lax.Precision.HIGHEST)
    tap_count = per_block.shape[0]
    block_count = per_block.shape[1]
    return jnp.broadcast_to(per_block[:, :, None], (tap_count, block_count, BLK)).reshape(
        tap_count, block_count * BLK
    )


def data_gradient(values, target, row_coef, col_coef):
    blurred = blur_line(values, row_coef, 1, False)
    columns = lax.all_to_all(blurred, "rows", split_axis=1, concat_axis=0, tiled=True)
    columns = blur_line(columns, col_coef, 0, False)
    if target is not None:
        columns = columns - target
    spread = blur_line(columns, col_coef, 0, True)
    back_rows = lax.all_to_all(spread, "rows", split_axis=0, concat_axis=1, tiled=True)
    return blur_line(back_rows, row_coef, 1, True)


def band_rims(values):
    return padded_2(values, (("rows", 1),), 1)


def denoise(data_step, cotangent, w_first, w_mid, w_last, add_rims, rim_dim):
    first_in = data_step.astype(jnp.bfloat16)[None]
    first_pad = add_rims(first_in)
    pre_first = conv_rim(first_pad, w_first)
    act_first = jax.nn.silu(pre_first).astype(jnp.bfloat16)
    first_act_pad = add_rims(act_first)
    pre_mid = conv_rim(first_act_pad, w_mid)
    act_mid = jax.nn.silu(pre_mid).astype(jnp.bfloat16)
    mid_act_pad = add_rims(act_mid)
    denoised = data_step + conv_rim(mid_act_pad, w_last)[0]
    cot_in = cotangent.astype(jnp.bfloat16)[None]
    cot_pad = add_rims(cot_in)
    back_mid = (conv_rim(cot_pad, flipped(w_last)) * silu_slope(pre_mid)).astype(jnp.bfloat16)
    back_mid_pad = add_rims(back_mid)
    back_first = (conv_rim(back_mid_pad, flipped(w_mid)) * silu_slope(pre_first)).astype(
        jnp.bfloat16
    )
    back_first_pad = add_rims(back_first)
    grad_data = cotangent + conv_rim(back_first_pad, flipped(w_first))[0]
    grad_last = weight_grad(mid_act_pad, cot_in, rim_dim)
    grad_mid = weight_grad(first_act_pad, back_mid, rim_dim)
    grad_first = weight_grad(first_pad, back_first, rim_dim)
    return (denoised, grad_data, (grad_first, grad_mid, grad_last))


def on_device(estimate, observed, cotangent, zone_map, bank_pick, psf_bank, w_first, w_mid, w_last):
    band_rows = estimate.shape[0]
    width = estimate.shape[1]
    group_cols = observed.shape[1]
    position = lax.axis_index("rows")
    height = band_rows * lax.axis_size("rows")
    kernels = zone_kernels(psf_bank, bank_pick)
    col_line = lax.dynamic_slice_in_dim(zone_map, position * group_cols // BLK, 1, 1)[:, 0]
    col_coef = tap_table(col_line, kernels[1])
    row_line = lax.dynamic_slice_in_dim(zone_map, position * band_rows // BLK, 1, 0)[0]
    row_coef = tap_table(row_line, kernels[0])
    data_step = estimate - STEP_SIZE * data_gradient(estimate, observed, row_coef, col_coef)
    denoised, grad_data, partial_grads = denoise(
        data_step, cotangent, w_first, w_mid, w_last, band_rims, 1
    )
    grad_estimate = grad_data - STEP_SIZE * data_gradient(grad_data, None, row_coef, col_coef)
    grad_scale = GRAD_FACTOR / math.sqrt(height * width)
    grad_first, grad_mid, grad_last = lax.psum(
        (
            partial_grads[0] * grad_scale,
            partial_grads[1] * grad_scale,
            partial_grads[2] * grad_scale,
        ),
        "rows",
    )
    return (denoised, grad_estimate, grad_first, grad_mid, grad_last)


def solution(mesh):
    placed = (
        P(("parts", "rows"), None),
        P("parts", "rows"),
        P(("parts", "rows"), None),
        P("parts", None),
        P(),
        P(),
        P(),
        P(),
        P(),
    )
    return jax.shard_map(
        on_device,
        mesh=mesh,
        in_specs=placed,
        out_specs=(
            P(("parts", "rows"), None),
            P(("parts", "rows"), None),
            P("parts", None, None, None),
            P("parts", None, None, None),
            P("parts", None, None, None),
        ),
        check_vma=False,
    )
```

profile of v0, /device:TPU:0, one launch (start us, length us, event | category | flops | bytes accessed | tf_op | source)
XLA Modules:
  0.0 456.3 jit_solution(8213222737690068692)
XLA Ops:
  13.1 9.3 %all-to-all-start = ((f32[8,16,128]{2,0,1:T(8,128)}), f32[8,16,128]{2,0,1:T(8,128)S(1)}, u32[]{:S(2)}, u32[]{:S(2)}) async-start(f32[8,16,128]{2,0,1:T(8,128)} %add_bitcast_fusion.1), calls=%async_computation | async-start | bytes 131072 | tf_op jit(solution)/shard_map/all_to_all | solution.py:111
  29.3 16.7 %broadcast_multiply_fusion.47 = (f32[128,128]{1,0:T(8,128)S(1)}, f32[128,128]{1,0:T(8,128)S(1)}) fusion(f32[]{:T(128)} %bitcast.9, f32[128,128]{1,0:T(8,128)} %param.10, f32[]{:T(128)} %bitcast.61, f32[]{:T(128)} %bitcast.60, f32[]{:T(128)} %bitcast.59, f32[]{:T(128)} %bitcast.58, f32[]{:T(128)} %bitcast.57, f32[]{:T(128)} %bitcast.56, f32[]{:T(128)} %bitcast.55, ...), kind=kLoop, calls=%fused_computation.672 | loop fusion | flops 835584 | bytes 262244 | tf_op jit(solution)/shard_map/mul | solution.py:79
  49.4 11.4 %broadcast_multiply_fusion.45 = (f32[128,128]{1,0:T(8,128)S(1)}, f32[128,128]{1,0:T(8,128)S(1)}, f32[128,128]{1,0:T(8,128)S(1)}, f32[128,128]{1,0:T(8,128)S(1)},...) fusion(f32[128,128]{1,0:T(8,128)S(1)} %get-tuple-element.38, ...), kind=kLoop, calls=%fused_computation.670 | loop fusion | flops 294912 | bytes 1245256 | tf_op jit(solution)/shard_map/mul | solution.py:79
  78.0 7.6 %fusion.358 = f32[8,8,257,32]{3,1,2,0:T(8,128)} fusion(bf16[1,10,8,259]{2,0,3,1:T(2,128)(2,1)S(1)} %copy.104, bf16[32,1,3,3]{0,3,2,1:T(4,128)(2,1)S(1)} %bitcast.471), kind=kOutput, calls=%fused_computation.709 | convolution fusion | flops 9474048 | bytes 2147360 | tf_op jit(solution)/shard_map/conv_general_dilated | solution.py:37
  85.6 7.2 %copy.106 = f32[8,8,257,32]{2,3,1,0:T(8,128)} copy(f32[8,8,257,32]{3,1,2,0:T(8,128)} %fusion.358) | data formatting | bytes 4210688 | tf_op jit(solution)/shard_map/conv_general_dilated | solution.py:37
  95.1 7.6 %fusion.361 = f32[8,8,257,32]{3,1,2,0:T(8,128)} fusion(bf16[1,10,8,259]{2,0,3,1:T(2,128)(2,1)S(1)} %copy.92, bf16[32,1,3,3]{0,3,2,1:T(4,128)(2,1)S(1)} %copy-done.80), kind=kOutput, calls=%fused_computation.712 | convolution fusion | flops 9474048 | bytes 2147360 | tf_op jit(solution)/shard_map/conv_general_dilated | solution.py:37
  102.7 5.9 %copy.94 = f32[8,8,257,32]{2,3,1,0:T(8,128)S(1)} copy(f32[8,8,257,32]{3,1,2,0:T(8,128)} %fusion.361) | data formatting | bytes 4210688 | tf_op jit(solution)/shard_map/conv_general_dilated | solution.py:37
  131.8 7.5 %copy.97 = bf16[32,10,1,8,257]{0,3,4,1,2:T(8,128)(2,1)} copy(bf16[32,10,1,8,257]{4,3,0,1,2:T(8,128)(2,1)} %reshape.468) | data formatting | bytes 2631680 | tf_op jit(solution)/shard_map/conv_general_dilated | solution.py:37
  140.2 11.1 %fusion.6 = f32[8,8,257,32]{3,1,2,0:T(8,128)} fusion(bf16[32,32,3,3]{1,0,3,2:T(8,128)(2,1)S(1)} %copy-done, bf16[32,10,1,7,2]{0,3,4,1,2:T(8,128)(2,1)S(1)} %slice.1495, bf16[32,10,1,8,257]{0,3,4,1,2:T(8,128)(2,1)} %copy.97), kind=kOutput, calls=%fused_computation.7 | convolution fusion | flops 307147776 | bytes 3448576 | tf_op jit(solution)/shard_map/conv_general_dilated | solution.py:37
  151.2 7.1 %copy.98 = f32[8,8,257,32]{2,3,1,0:T(8,128)} copy(f32[8,8,257,32]{3,1,2,0:T(8,128)} %fusion.6) | data formatting | bytes 4210688 | tf_op jit(solution)/shard_map/conv_general_dilated | solution.py:37
  158.3 6.4 %multiply_convert_fusion.1 = (bf16[8,8,257,32]{2,3,1,0:T(8,128)(2,1)}, f32[8,8,257,32]{2,3,1,0:T(8,128)S(1)}, f32[8,8,257,32]{2,3,1,0:T(8,128)}) fusion(f32[8,8,257,32]{2,3,1,0:T(8,128)} %copy.98, pred[8,257]{1,0:T(8,128)(4,1)S(1)} %copy-done.79, f32[8,8,257,32]{2,3,1,0:T(8,128)} %copy.106), kind=kLoop, calls=%fused_computation.32 | loop fusion | flops 5789696 | bytes 9476104 | tf_op jit(solution)/shard_map/convert_element_type | solution.py:136
  196.1 6.1 %collective-permute-start.4 = (bf16[32,1,2048]{2,0,1:T(8,128)(2,1)}, bf16[32,1,2048]{2,0,1:T(8,128)(2,1)}, u32[]{:S(2)}, u32[]{:S(2)}) collective-permute-start(bf16[32,1,2048]{2,0,1:T(8,128)(2,1)} %get-tuple-element.55), channel_id=1, source_target_pairs={{0,1},{1,2},{2,3},{3,4},{4,5},{5,6},{6,7},{7,8},{8,9},{9,10},{10,1... | collective-permute-start | bytes 393224 | tf_op jit(solution)/shard_map/ppermute | solution.py:20
  221.4 7.5 %copy.101 = bf16[32,10,1,8,257]{0,3,4,1,2:T(8,128)(2,1)} copy(bf16[32,10,1,8,257]{4,3,0,1,2:T(8,128)(2,1)} %reshape.475) | data formatting | bytes 2631680 | tf_op jit(solution)/shard_map/conv_general_dilated | solution.py:37
  229.8 11.8 %broadcast_select_fusion.1 = f32[8,8,257,1]{3,1,2,0:T(8,128)} fusion(pred[8,257]{0,1:T(8,128)(4,1)S(1)} %copy-done.82, bf16[32,10,1,7,2]{0,3,4,1,2:T(8,128)(2,1)S(1)} %slice.1499, bf16[32,10,1,8,257]{0,3,4,1,2:T(8,128)(2,1)} %copy.101, bf16[1,32,3,3]{1,3,2,0:T(4,128)(2,1)S(1)} %copy-done.81), kind=kOutput, calls=%fused_computation.30 | convolution fusion | flops 13468736 | bytes 1393224 | tf_op jit(solution)/shard_map/conv_general_dilated | solution.py:37
  241.5 6.1 %copy.103 = f32[8,8,257,1]{2,1,0,3:T(8,128)S(1)} copy(f32[8,8,257,1]{3,1,2,0:T(8,128)} %broadcast_select_fusion.1) | data formatting | bytes 131584 | tf_op jit(solution)/shard_map/conv_general_dilated | solution.py:37
  254.5 11.2 %fusion.14 = f32[8,8,257,32]{3,1,2,0:T(8,128)} fusion(bf16[32,32,3,3]{1,0,3,2:T(8,128)(2,1)S(1)} %copy-done, bf16[32,10,1,7,2]{0,3,4,1,2:T(8,128)(2,1)S(1)} %slice.1507, bf16[32,10,1,8,257]{0,3,4,1,2:T(8,128)(2,1)} %copy.109), kind=kOutput, calls=%fused_computation.13 | convolution fusion | flops 307147776 | bytes 3448576 | tf_op jit(solution)/shard_map/conv_general_dilated | solution.py:37
  265.7 7.3 %copy.110 = f32[8,8,257,32]{2,3,1,0:T(8,128)} copy(f32[8,8,257,32]{3,1,2,0:T(8,128)} %fusion.14) | data formatting | bytes 4210688 | tf_op jit(solution)/shard_map/conv_general_dilated | solution.py:37
  273.0 5.6 %multiply_convert_fusion.2 = (bf16[8,8,257,32]{2,3,1,0:T(8,128)(2,1)S(1)}, bf16[8,8,257,32]{2,3,1,0:T(8,128)(2,1)}, f32[8,8,257,32]{2,3,1,0:T(8,128)}) fusion(f32[8,8,257,32]{2,3,1,0:T(8,128)S(1)} %copy-done.2, pred[8,257]{1,0:T(8,128)(4,1)S(1)} %copy-done.79, f32[8,8,257,32]{2,3,1,0:T(8,128)} %copy.110), kind=kLoop, calls=%fused_computation.33 | loop fusion | flops 6842368 | bytes 8423432 | tf_op jit(solution)/shard_map/convert_element_type | solution.py:128
  315.8 11.8 %broadcast_select_fusion = f32[8,8,257,1]{3,1,2,0:T(8,128)} fusion(pred[8,257]{0,1:T(8,128)(4,1)S(1)} %copy-done.83, bf16[32,10,1,7,2]{0,3,4,1,2:T(8,128)(2,1)S(1)} %slice.1511, bf16[32,10,1,8,257]{0,3,4,1,2:T(8,128)(2,1)} %copy.113, bf16[1,32,3,3]{1,3,2,0:T(4,128)(2,1)S(1)} %bitcast.470), kind=kOutput, calls=%fused_computation.29 | convolution fusion | flops 13468736 | bytes 1393224 | tf_op jit(solution)/shard_map/conv_general_dilated | solution.py:37
  327.6 6.3 %copy.115 = f32[8,8,257,1]{2,1,0,3:T(8,128)S(1)} copy(f32[8,8,257,1]{3,1,2,0:T(8,128)} %broadcast_select_fusion) | data formatting | bytes 131584 | tf_op jit(solution)/shard_map/conv_general_dilated | solution.py:37
  339.3 8.8 %all-to-all-start.2 = ((f32[8,16,128]{2,0,1:T(8,128)}), f32[8,16,128]{2,0,1:T(8,128)S(1)}, u32[]{:S(2)}, u32[]{:S(2)}) async-start(f32[8,16,128]{2,0,1:T(8,128)} %add_bitcast_fusion), calls=%async_computation.2 | async-start | bytes 131072 | tf_op jit(solution)/shard_map/all_to_all | solution.py:111
  355.1 15.9 %broadcast_multiply_fusion.46 = (f32[128,128]{1,0:T(8,128)S(1)}, f32[128,128]{1,0:T(8,128)S(1)}) fusion(f32[]{:T(128)} %bitcast.9, f32[]{:T(128)} %bitcast.61, f32[]{:T(128)} %bitcast.60, f32[]{:T(128)} %bitcast.59, f32[]{:T(128)} %bitcast.58, f32[]{:T(128)} %bitcast.57, f32[]{:T(128)} %bitcast.56, f32[]{:T(128)} %bitcast.55, f32[]{:T(128)} %bitcast.54, ...), kind=kLoop, calls=%fused_computation.671 | loop fusion | flops 819200 | bytes 196708 | tf_op jit(solution)/shard_map/mul | solution.py:79
  374.3 11.4 %broadcast_multiply_fusion.44 = (f32[128,128]{1,0:T(8,128)S(1)}, f32[128,128]{1,0:T(8,128)S(1)}, f32[128,128]{1,0:T(8,128)S(1)}, f32[128,128]{1,0:T(8,128)S(1)},...) fusion(f32[128,128]{1,0:T(8,128)S(1)} %get-tuple-element.36, ...), kind=kLoop, calls=%fused_computation.669 | loop fusion | flops 294912 | bytes 1245256 | tf_op jit(solution)/shard_map/mul | solution.py:79
  390.7 64.1 %all-reduce.103 = (f32[32,1,3,3]{0,1,3,2:T(1,128)}, f32[32,32,3,3]{1,0,3,2:T(8,128)}, f32[1,32,3,3]{1,0,3,2:T(1,128)}) all-reduce(f32[32,1,3,3]{0,1,3,2:T(1,128)S(1)} %maximum_multiply_fusion.1, f32[32,32,3,3]{1,0,3,2:T(8,128)S(1)} %copy-done.14, ...), channel_id=1, replica_groups=mesh['parts'=2,'rows'=16] {'rows'}, use_global_device_ids=true, to_apply=%region_1.2 | all-reduce | flops 9792 | bytes 78336 | tf_op jit(solution)/shard_map/psum | solution.py:166
  (340 shorter events, 182.2 us)
Async XLA Ops:
  0.6 139.5 %copy-start = (bf16[32,32,3,3]{1,0,3,2:T(8,128)(2,1)S(1)}, bf16[32,32,3,3]{1,0,3,2:T(8,128)(2,1)}, u32[]{:S(2)}) copy-start(bf16[32,32,3,3]{1,0,3,2:T(8,128)(2,1)} %param.16) | copy-start | bytes 55300
  1.5 64.8 %collective-permute-start.6 = (bf16[1,1,2048]{2,1,0:T(2,128)(2,1)S(1)}, bf16[1,1,2048]{2,1,0:T(2,128)(2,1)S(1)}, u32[]{:S(2)}, u32[]{:S(2)}) collective-permute-start(bf16[1,1,2048]{2,1,0:T(2,128)(2,1)S(1)} %get-tuple-element.165), channel_id=1, source_target_pairs={{0,1},{1,2},{2,3},{3,4},{4,5},{5,6},{6,7},{7,8},{8,9},{9,10},{10,1... | collective-permute-start | bytes 12296 | tf_op jit(solution)/shard_map/ppermute | solution.py:20
  3.9 62.4 %collective-permute-start.7 = (bf16[1,1,2048]{2,1,0:T(2,128)(2,1)S(1)}, bf16[1,1,2048]{2,1,0:T(2,128)(2,1)S(1)}, u32[]{:S(2)}, u32[]{:S(2)}) collective-permute-start(bf16[1,1,2048]{2,1,0:T(2,128)(2,1)S(1)} %get-tuple-element.166), channel_id=1, source_target_pairs={{1,0},{2,1},{3,2},{4,3},{5,4},{6,5},{7,6},{8,7},{9,8},{10,9},{11,1... | collective-permute-start | bytes 12296 | tf_op jit(solution)/shard_map/ppermute | solution.py:21
  8.6 64.7 %copy-start.17 = (f32[2048]{0:T(1024)}, f32[2048]{0:T(1024)S(1)}, u32[]{:S(2)}) copy-start(f32[2048]{0:T(1024)S(1)} %broadcast_bitcast_fusion.24) | copy-start | bytes 24580
  8.7 64.6 %copy-start.19 = (f32[2048]{0:T(1024)}, f32[2048]{0:T(1024)S(1)}, u32[]{:S(2)}) copy-start(f32[2048]{0:T(1024)S(1)} %get-tuple-element.216) | copy-start | bytes 24580
  8.7 64.6 %copy-start.21 = (f32[2048]{0:T(1024)}, f32[2048]{0:T(1024)S(1)}, u32[]{:S(2)}) copy-start(f32[2048]{0:T(1024)S(1)} %get-tuple-element.217) | copy-start | bytes 24580
  8.7 64.5 %copy-start.39 = (f32[2048]{0:T(1024)}, f32[2048]{0:T(1024)S(1)}, u32[]{:S(2)}) copy-start(f32[2048]{0:T(1024)S(1)} %get-tuple-element.194) | copy-start | bytes 24580
  8.7 64.5 %copy-start.41 = (f32[2048]{0:T(1024)}, f32[2048]{0:T(1024)S(1)}, u32[]{:S(2)}) copy-start(f32[2048]{0:T(1024)S(1)} %get-tuple-element.195) | copy-start | bytes 24580
  8.8 64.4 %copy-start.49 = (f32[2048]{0:T(1024)}, f32[2048]{0:T(1024)S(1)}, u32[]{:S(2)}) copy-start(f32[2048]{0:T(1024)S(1)} %get-tuple-element.197) | copy-start | bytes 24580
  9.2 64.4 %copy-start.23 = (f32[2048]{0:T(1024)}, f32[2048]{0:T(1024)S(1)}, u32[]{:S(2)}) copy-start(f32[2048]{0:T(1024)S(1)} %get-tuple-element.206) | copy-start | bytes 24580
  13.1 16.2 %all-to-all-start = ((f32[8,16,128]{2,0,1:T(8,128)}), f32[8,16,128]{2,0,1:T(8,128)S(1)}, u32[]{:S(2)}, u32[]{:S(2)}) async-start(f32[8,16,128]{2,0,1:T(8,128)} %add_bitcast_fusion.1), calls=%async_computation | async-start | bytes 131072 | tf_op jit(solution)/shard_map/all_to_all | solution.py:111
  62.2 11.0 %all-to-all-start.1 = ((f32[16,8,128]{2,1,0:T(8,128)}), f32[16,8,128]{2,1,0:T(8,128)S(1)}, u32[]{:S(2)}, u32[]{:S(2)}) async-start(f32[16,8,128]{2,1,0:T(8,128)} %fusion.342), calls=%async_computation.1 | async-start | bytes 131072 | tf_op jit(solution)/shard_map/all_to_all | solution.py:116
  74.8 18.0 %collective-permute-start = (bf16[1,1,2048]{2,1,0:T(2,128)(2,1)S(1)}, bf16[1,1,2048]{2,1,0:T(2,128)(2,1)S(1)}, u32[]{:S(2)}, u32[]{:S(2)}) collective-permute-start(bf16[1,1,2048]{2,1,0:T(2,128)(2,1)S(1)} %get-tuple-element.167), channel_id=1, source_target_pairs={{0,1},{1,2},{2,3},{3,4},{4,5},{5,6},{6,7},{7,8},{8,9},{9,10},{10,1... | collective-permute-start | bytes 12296 | tf_op jit(solution)/shard_map/ppermute | solution.py:20
  76.2 16.5 %collective-permute-start.1 = (bf16[1,1,2048]{2,1,0:T(2,128)(2,1)S(1)}, bf16[1,1,2048]{2,1,0:T(2,128)(2,1)S(1)}, u32[]{:S(2)}, u32[]{:S(2)}) collective-permute-start(bf16[1,1,2048]{2,1,0:T(2,128)(2,1)S(1)} %get-tuple-element.168), channel_id=1, source_target_pairs={{1,0},{2,1},{3,2},{4,3},{5,4},{6,5},{7,6},{8,7},{9,8},{10,9},{11,1... | collective-permute-start | bytes 12296 | tf_op jit(solution)/shard_map/ppermute | solution.py:21
  117.3 5.2 %collective-permute-start.2 = (bf16[32,1,2048]{2,0,1:T(8,128)(2,1)S(1)}, bf16[32,1,2048]{2,0,1:T(8,128)(2,1)S(1)}, u32[]{:S(2)}, u32[]{:S(2)}) collective-permute-start(bf16[32,1,2048]{2,0,1:T(8,128)(2,1)S(1)} %get-tuple-element.57), channel_id=1, source_target_pairs={{0,1},{1,2},{2,3},{3,4},{4,5},{5,6},{6,7},{7,8},{8,9},{9,10},{10,1... | collective-permute-start | bytes 393224 | tf_op jit(solution)/shard_map/ppermute | solution.py:20
  120.6 4.5 collective-permute-start.3
  196.1 18.9 %collective-permute-start.4 = (bf16[32,1,2048]{2,0,1:T(8,128)(2,1)}, bf16[32,1,2048]{2,0,1:T(8,128)(2,1)}, u32[]{:S(2)}, u32[]{:S(2)}) collective-permute-start(bf16[32,1,2048]{2,0,1:T(8,128)(2,1)} %get-tuple-element.55), channel_id=1, source_target_pairs={{0,1},{1,2},{2,3},{3,4},{4,5},{5,6},{6,7},{7,8},{8,9},{9,10},{10,1... | collective-permute-start | bytes 393224 | tf_op jit(solution)/shard_map/ppermute | solution.py:20
  202.2 12.8 %collective-permute-start.5 = (bf16[32,1,2048]{2,0,1:T(8,128)(2,1)}, bf16[32,1,2048]{2,0,1:T(8,128)(2,1)}, u32[]{:S(2)}, u32[]{:S(2)}) collective-permute-start(bf16[32,1,2048]{2,0,1:T(8,128)(2,1)} %get-tuple-element.56), channel_id=1, source_target_pairs={{1,0},{2,1},{3,2},{4,3},{5,4},{6,5},{7,6},{8,7},{9,8},{10,9},{11,1... | collective-permute-start | bytes 393224 | tf_op jit(solution)/shard_map/ppermute | solution.py:21
  203.5 7.0 %collective-permute-start.8 = (bf16[32,1,2048]{2,0,1:T(8,128)(2,1)}, bf16[32,1,2048]{2,0,1:T(8,128)(2,1)S(1)}, u32[]{:S(2)}, u32[]{:S(2)}) collective-permute-start(bf16[32,1,2048]{2,0,1:T(8,128)(2,1)} %get-tuple-element.53), channel_id=1, source_target_pairs={{0,1},{1,2},{2,3},{3,4},{4,5},{5,6},{6,7},{7,8},{8,9},{9,10},{10,1... | collective-permute-start | bytes 393224 | tf_op jit(solution)/shard_map/ppermute | solution.py:20
  206.5 5.0 %collective-permute-start.9 = (bf16[32,1,2048]{2,0,1:T(8,128)(2,1)S(1)}, bf16[32,1,2048]{2,0,1:T(8,128)(2,1)S(1)}, u32[]{:S(2)}, u32[]{:S(2)}) collective-permute-start(bf16[32,1,2048]{2,0,1:T(8,128)(2,1)S(1)} %get-tuple-element.54), channel_id=1, source_target_pairs={{1,0},{2,1},{3,2},{4,3},{5,4},{6,5},{7,6},{8,7},{9,8},{10,9},{11,1... | collective-permute-start | bytes 393224 | tf_op jit(solution)/shard_map/ppermute | solution.py:21
  297.8 7.9 %collective-permute-start.10 = (bf16[32,1,2048]{2,0,1:T(8,128)(2,1)S(1)}, bf16[32,1,2048]{2,0,1:T(8,128)(2,1)S(1)}, u32[]{:S(2)}, u32[]{:S(2)}) collective-permute-start(bf16[32,1,2048]{2,0,1:T(8,128)(2,1)S(1)} %get-tuple-element.51), channel_id=1, source_target_pairs={{0,1},{1,2},{2,3},{3,4},{4,5},{5,6},{6,7},{7,8},{8,9},{9,10},{10,1... | collective-permute-start | bytes 393224 | tf_op jit(solution)/shard_map/ppermute | solution.py:20
  303.3 3.2 collective-permute-start.11
  339.3 15.8 %all-to-all-start.2 = ((f32[8,16,128]{2,0,1:T(8,128)}), f32[8,16,128]{2,0,1:T(8,128)S(1)}, u32[]{:S(2)}, u32[]{:S(2)}) async-start(f32[8,16,128]{2,0,1:T(8,128)} %add_bitcast_fusion), calls=%async_computation.2 | async-start | bytes 131072 | tf_op jit(solution)/shard_map/all_to_all | solution.py:111
  387.1 67.7 %all-to-all-start.3 = ((f32[16,8,128]{2,1,0:T(8,128)}), f32[16,8,128]{2,1,0:T(8,128)S(1)}, u32[]{:S(2)}, u32[]{:S(2)}) async-start(f32[16,8,128]{2,1,0:T(8,128)} %fusion.341), calls=%async_computation.3 | async-start | bytes 131072 | tf_op jit(solution)/shard_map/all_to_all | solution.py:116
  (76 other events, 1404.0 us)
where the time goes:
time: 463 us; the launch traced here: 456 us
  local copies, waits for them, and re-layouts  139 us (30%)
  other arithmetic  99.6 us (22%)
  matrix products  80.2 us (17%)
  blocking collectives  64.1 us (14%)
  starting transfers between devices  55.6 us (12%)
  waiting for transfers between devices  15.9 us (3%)
    conv_general_dilated x34, local copies, waits for them, and re-layouts, conv_rim(): lax.conv_general_dilated(padded[None], weight, (1, 1), padding, dimension...  116 us
    psum x1, blocking collectives, on_device(): lax.psum((partial_grads[0] * grad_scale, partial_grads[1] * grad_scale, p...  64.1 us
    mul x10, other arithmetic, blur_line(): spread = jnp.pad(factor * values, widths)  62.5 us
    conv_general_dilated x6, matrix products, conv_rim(): lax.conv_general_dilated(padded[None], weight, (1, 1), padding, dimension...  61 us
    ppermute x6, starting transfers between devices, padded_2(): before = lax.ppermute(last, axis, up)  21.6 us
    all_to_all x2, starting transfers between devices, data_gradient(): lax.all_to_all(blurred, 'rows', split_axis=1, concat_axis=0, tiled=True)  18.1 us
    dot_general x27, matrix products, weight_taps(): jnp.einsum('ohw,chw->oc', errors, window, preferred_element_type=jnp.floa...  16.8 us
    convert_element_type x2, other arithmetic, denoise(): (conv_rim(cot_pad, flipped(w_last)) * silu_slope(pre_mid)).astype(jnp.bfl...  10.5 us
  transfers between devices with their start and end apart: 16, of which 6 were waited for; matrix products, arithmetic and copies ran while one was open for 16% of the time, Pallas kernels for 0%

commit v1 on v0

--- a/solution.py
+++ b/solution.py
@@ -8,6 +8,12 @@
 RAD = 12
 STEP_SIZE = 2.0
 GRAD_FACTOR = 8.0
+
+
+def trade_parts(x, axis, split, join):
+    cells = jnp.split(x, lax.axis_size(axis), axis=split)
+    got = lax.all_to_all(jnp.stack(cells), axis, 0, 0)
+    return jnp.concatenate(got, axis=join)
 
 
 def padded_2(shard, sides, width):
@@ -108,7 +114,7 @@
 
 def data_gradient(values, target, row_coef, col_coef):
     blurred = blur_line(values, row_coef, 1, False)
-    columns = lax.all_to_all(blurred, "rows", split_axis=1, concat_axis=0, tiled=True)
+    columns = trade_parts(blurred, "rows", 1, 0)
     columns = blur_line(columns, col_coef, 0, False)
     if target is not None:
         columns = columns - target

time: 463 us -> 481 us (1.039)
  local copies, waits for them, and re-layouts: 139 us -> 158 us
    unnamed x168 -> x198, local copies, waits for them, and re-layouts: 2.41 us -> 20.2 us
  transfers between devices with their start and end apart: 16 -> 16, of which waited for: 6 -> 6; matrix products, arithmetic and copies ran while one was open for 16% -> 17% of each run, Pallas kernels for 0% -> 0%
where the time goes in v1:
time: 481 us; the launch traced here: 474 us
  local copies, waits for them, and re-layouts  158 us (33%)
  other arithmetic  98.4 us (20%)
  matrix products  80.2 us (17%)
  blocking collectives  64.1 us (13%)
  starting transfers between devices  55.6 us (12%)
  waiting for transfers between devices  15.9 us (3%)
    conv_general_dilated x34, local copies, waits for them, and re-layouts, conv_rim(): lax.conv_general_dilated(padded[None], weight, (1, 1), padding, dimension...  116 us
    psum x1, blocking collectives, on_device(): lax.psum((partial_grads[0] * grad_scale, partial_grads[1] * grad_scale, p...  64.1 us
    mul x10, other arithmetic, blur_line(): spread = jnp.pad(factor * values, widths)  62.5 us
    conv_general_dilated x6, matrix products, conv_rim(): lax.conv_general_dilated(padded[None], weight, (1, 1), padding, dimension...  61 us
    ppermute x6, starting transfers between devices, padded_2(): before = lax.ppermute(last, axis, up)  21.6 us
    unnamed x198, local copies, waits for them, and re-layouts  20.2 us
    all_to_all x2, starting transfers between devices, trade_parts(): got = lax.all_to_all(jnp.stack(cells), axis, 0, 0)  18.1 us
    dot_general x27, matrix products, weight_taps(): jnp.einsum('ohw,chw->oc', errors, window, preferred_element_type=jnp.floa...  16.8 us
  transfers between devices with their start and end apart: 16, of which 6 were waited for; matrix products, arithmetic and copies ran while one was open for 17% of the time, Pallas kernels for 0%

profile of v1, /device:TPU:0, one launch (start us, length us, event | category | flops | bytes accessed | tf_op | source)
XLA Modules:
  0.0 474.2 jit_solution(439270120725951630)
XLA Ops:
  22.0 9.3 %all-to-all-start = ((f32[16,8,128]{2,1,0:T(8,128)}), f32[16,8,128]{2,1,0:T(8,128)S(1)}, u32[]{:S(2)}, u32[]{:S(2)}) async-start(f32[16,8,128]{2,1,0:T(8,128)} %constant_dynamic-update-slice_fusion), calls=%async_computation | async-start | bytes 131072 | tf_op jit(solution)/shard_map/all_to_all | solution.py:15
  38.2 16.7 %broadcast_multiply_fusion.47 = (f32[128,128]{1,0:T(8,128)S(1)}, f32[128,128]{1,0:T(8,128)S(1)}) fusion(f32[]{:T(128)} %bitcast.9, f32[128,128]{1,0:T(8,128)} %param.10, f32[]{:T(128)} %bitcast.74, f32[]{:T(128)} %bitcast.73, f32[]{:T(128)} %bitcast.72, f32[]{:T(128)} %bitcast.71, f32[]{:T(128)} %bitcast.70, f32[]{:T(128)} %bitcast.69, f32[]{:T(128)} %bitcast.68, ...), kind=kLoop, calls=%fused_computation.704 | loop fusion | flops 835584 | bytes 262244 | tf_op jit(solution)/shard_map/mul | solution.py:85
  58.2 11.4 %broadcast_multiply_fusion.45 = (f32[128,128]{1,0:T(8,128)S(1)}, f32[128,128]{1,0:T(8,128)S(1)}, f32[128,128]{1,0:T(8,128)S(1)}, f32[128,128]{1,0:T(8,128)S(1)},...) fusion(f32[128,128]{1,0:T(8,128)S(1)} %get-tuple-element.38, ...), kind=kLoop, calls=%fused_computation.702 | loop fusion | flops 294912 | bytes 1245256 | tf_op jit(solution)/shard_map/mul | solution.py:85
  86.9 7.6 %fusion.358 = f32[8,8,257,32]{3,1,2,0:T(8,128)} fusion(bf16[1,10,8,259]{2,0,3,1:T(2,128)(2,1)S(1)} %copy.104, bf16[32,1,3,3]{0,3,2,1:T(4,128)(2,1)S(1)} %bitcast.591), kind=kOutput, calls=%fused_computation.741 | convolution fusion | flops 9474048 | bytes 2147360 | tf_op jit(solution)/shard_map/conv_general_dilated | solution.py:43
  94.5 7.2 %copy.106 = f32[8,8,257,32]{2,3,1,0:T(8,128)} copy(f32[8,8,257,32]{3,1,2,0:T(8,128)} %fusion.358) | data formatting | bytes 4210688 | tf_op jit(solution)/shard_map/conv_general_dilated | solution.py:43
  104.0 7.6 %fusion.361 = f32[8,8,257,32]{3,1,2,0:T(8,128)} fusion(bf16[1,10,8,259]{2,0,3,1:T(2,128)(2,1)S(1)} %copy.92, bf16[32,1,3,3]{0,3,2,1:T(4,128)(2,1)S(1)} %copy-done.80), kind=kOutput, calls=%fused_computation.744 | convolution fusion | flops 9474048 | bytes 2147360 | tf_op jit(solution)/shard_map/conv_general_dilated | solution.py:43
  111.6 5.9 %copy.94 = f32[8,8,257,32]{2,3,1,0:T(8,128)S(1)} copy(f32[8,8,257,32]{3,1,2,0:T(8,128)} %fusion.361) | data formatting | bytes 4210688 | tf_op jit(solution)/shard_map/conv_general_dilated | solution.py:43
  140.7 7.5 %copy.97 = bf16[32,10,1,8,257]{0,3,4,1,2:T(8,128)(2,1)} copy(bf16[32,10,1,8,257]{4,3,0,1,2:T(8,128)(2,1)} %reshape.470) | data formatting | bytes 2631680 | tf_op jit(solution)/shard_map/conv_general_dilated | solution.py:43
  149.0 11.1 %fusion.6 = f32[8,8,257,32]{3,1,2,0:T(8,128)} fusion(bf16[32,32,3,3]{1,0,3,2:T(8,128)(2,1)S(1)} %copy-done, bf16[32,10,1,7,2]{0,3,4,1,2:T(8,128)(2,1)S(1)} %slice.1495, bf16[32,10,1,8,257]{0,3,4,1,2:T(8,128)(2,1)} %copy.97), kind=kOutput, calls=%fused_computation.7 | convolution fusion | flops 307147776 | bytes 3448576 | tf_op jit(solution)/shard_map/conv_general_dilated | solution.py:43
  160.1 7.1 %copy.98 = f32[8,8,257,32]{2,3,1,0:T(8,128)} copy(f32[8,8,257,32]{3,1,2,0:T(8,128)} %fusion.6) | data formatting | bytes 4210688 | tf_op jit(solution)/shard_map/conv_general_dilated | solution.py:43
  167.2 6.4 %multiply_convert_fusion.1 = (bf16[8,8,257,32]{2,3,1,0:T(8,128)(2,1)}, f32[8,8,257,32]{2,3,1,0:T(8,128)S(1)}, f32[8,8,257,32]{2,3,1,0:T(8,128)}) fusion(f32[8,8,257,32]{2,3,1,0:T(8,128)} %copy.98, pred[8,257]{1,0:T(8,128)(4,1)S(1)} %copy-done.79, f32[8,8,257,32]{2,3,1,0:T(8,128)} %copy.106), kind=kLoop, calls=%fused_computation.32 | loop fusion | flops 5789696 | bytes 9476104 | tf_op jit(solution)/shard_map/convert_element_type | solution.py:142
  204.9 6.1 %collective-permute-start.4 = (bf16[32,1,2048]{2,0,1:T(8,128)(2,1)}, bf16[32,1,2048]{2,0,1:T(8,128)(2,1)}, u32[]{:S(2)}, u32[]{:S(2)}) collective-permute-start(bf16[32,1,2048]{2,0,1:T(8,128)(2,1)} %get-tuple-element.55), channel_id=1, source_target_pairs={{0,1},{1,2},{2,3},{3,4},{4,5},{5,6},{6,7},{7,8},{8,9},{9,10},{10,1... | collective-permute-start | bytes 393224 | tf_op jit(solution)/shard_map/ppermute | solution.py:26
  230.3 7.5 %copy.101 = bf16[32,10,1,8,257]{0,3,4,1,2:T(8,128)(2,1)} copy(bf16[32,10,1,8,257]{4,3,0,1,2:T(8,128)(2,1)} %reshape.477) | data formatting | bytes 2631680 | tf_op jit(solution)/shard_map/conv_general_dilated | solution.py:43
  238.6 11.8 %broadcast_select_fusion.1 = f32[8,8,257,1]{3,1,2,0:T(8,128)} fusion(pred[8,257]{0,1:T(8,128)(4,1)S(1)} %copy-done.82, bf16[32,10,1,7,2]{0,3,4,1,2:T(8,128)(2,1)S(1)} %slice.1499, bf16[32,10,1,8,257]{0,3,4,1,2:T(8,128)(2,1)} %copy.101, bf16[1,32,3,3]{1,3,2,0:T(4,128)(2,1)S(1)} %copy-done.81), kind=kOutput, calls=%fused_computation.30 | convolution fusion | flops 13468736 | bytes 1393224 | tf_op jit(solution)/shard_map/conv_general_dilated | solution.py:43
  250.4 6.1 %copy.103 = f32[8,8,257,1]{2,1,0,3:T(8,128)S(1)} copy(f32[8,8,257,1]{3,1,2,0:T(8,128)} %broadcast_select_fusion.1) | data formatting | bytes 131584 | tf_op jit(solution)/shard_map/conv_general_dilated | solution.py:43
  263.4 11.2 %fusion.14 = f32[8,8,257,32]{3,1,2,0:T(8,128)} fusion(bf16[32,32,3,3]{1,0,3,2:T(8,128)(2,1)S(1)} %copy-done, bf16[32,10,1,7,2]{0,3,4,1,2:T(8,128)(2,1)S(1)} %slice.1507, bf16[32,10,1,8,257]{0,3,4,1,2:T(8,128)(2,1)} %copy.109), kind=kOutput, calls=%fused_computation.13 | convolution fusion | flops 307147776 | bytes 3448576 | tf_op jit(solution)/shard_map/conv_general_dilated | solution.py:43
  274.6 7.3 %copy.110 = f32[8,8,257,32]{2,3,1,0:T(8,128)} copy(f32[8,8,257,32]{3,1,2,0:T(8,128)} %fusion.14) | data formatting | bytes 4210688 | tf_op jit(solution)/shard_map/conv_general_dilated | solution.py:43
  281.8 5.6 %multiply_convert_fusion.2 = (bf16[8,8,257,32]{2,3,1,0:T(8,128)(2,1)S(1)}, bf16[8,8,257,32]{2,3,1,0:T(8,128)(2,1)}, f32[8,8,257,32]{2,3,1,0:T(8,128)}) fusion(f32[8,8,257,32]{2,3,1,0:T(8,128)S(1)} %copy-done.2, pred[8,257]{1,0:T(8,128)(4,1)S(1)} %copy-done.79, f32[8,8,257,32]{2,3,1,0:T(8,128)} %copy.110), kind=kLoop, calls=%fused_computation.33 | loop fusion | flops 6842368 | bytes 8423432 | tf_op jit(solution)/shard_map/convert_element_type | solution.py:134
  324.7 11.8 %broadcast_select_fusion = f32[8,8,257,1]{3,1,2,0:T(8,128)} fusion(pred[8,257]{0,1:T(8,128)(4,1)S(1)} %copy-done.83, bf16[32,10,1,7,2]{0,3,4,1,2:T(8,128)(2,1)S(1)} %slice.1511, bf16[32,10,1,8,257]{0,3,4,1,2:T(8,128)(2,1)} %copy.113, bf16[1,32,3,3]{1,3,2,0:T(4,128)(2,1)S(1)} %bitcast.590), kind=kOutput, calls=%fused_computation.29 | convolution fusion | flops 13468736 | bytes 1393224 | tf_op jit(solution)/shard_map/conv_general_dilated | solution.py:43
  336.5 6.3 %copy.115 = f32[8,8,257,1]{2,1,0,3:T(8,128)S(1)} copy(f32[8,8,257,1]{3,1,2,0:T(8,128)} %broadcast_select_fusion) | data formatting | bytes 131584 | tf_op jit(solution)/shard_map/conv_general_dilated | solution.py:43
  357.1 8.8 %all-to-all-start.2 = ((f32[16,8,128]{2,1,0:T(8,128)}), f32[16,8,128]{2,1,0:T(8,128)S(1)}, u32[]{:S(2)}, u32[]{:S(2)}) async-start(f32[16,8,128]{2,1,0:T(8,128)} %constant_dynamic-update-slice_fusion.16), calls=%async_computation.2 | async-start | bytes 131072 | tf_op jit(solution)/shard_map/all_to_all | solution.py:15
  372.9 15.9 %broadcast_multiply_fusion.46 = (f32[128,128]{1,0:T(8,128)S(1)}, f32[128,128]{1,0:T(8,128)S(1)}) fusion(f32[]{:T(128)} %bitcast.9, f32[]{:T(128)} %bitcast.74, f32[]{:T(128)} %bitcast.73, f32[]{:T(128)} %bitcast.72, f32[]{:T(128)} %bitcast.71, f32[]{:T(128)} %bitcast.70, f32[]{:T(128)} %bitcast.69, f32[]{:T(128)} %bitcast.68, f32[]{:T(128)} %bitcast.67, ...), kind=kLoop, calls=%fused_computation.703 | loop fusion | flops 819200 | bytes 196708 | tf_op jit(solution)/shard_map/mul | solution.py:85
  392.1 11.4 %broadcast_multiply_fusion.44 = (f32[128,128]{1,0:T(8,128)S(1)}, f32[128,128]{1,0:T(8,128)S(1)}, f32[128,128]{1,0:T(8,128)S(1)}, f32[128,128]{1,0:T(8,128)S(1)},...) fusion(f32[128,128]{1,0:T(8,128)S(1)} %get-tuple-element.36, ...), kind=kLoop, calls=%fused_computation.701 | loop fusion | flops 294912 | bytes 1245256 | tf_op jit(solution)/shard_map/mul | solution.py:85
  408.5 64.1 %all-reduce.103 = (f32[32,1,3,3]{0,1,3,2:T(1,128)}, f32[32,32,3,3]{1,0,3,2:T(8,128)}, f32[1,32,3,3]{1,0,3,2:T(1,128)}) all-reduce(f32[32,1,3,3]{0,1,3,2:T(1,128)S(1)} %maximum_multiply_fusion.1, f32[32,32,3,3]{1,0,3,2:T(8,128)S(1)} %copy-done.14, ...), channel_id=1, replica_groups=mesh['parts'=2,'rows'=16] {'rows'}, use_global_device_ids=true, to_apply=%region_1.2 | all-reduce | flops 9792 | bytes 78336 | tf_op jit(solution)/shard_map/psum | solution.py:172
  (372 shorter events, 200.0 us)
Async XLA Ops:
  0.6 148.4 %copy-start = (bf16[32,32,3,3]{1,0,3,2:T(8,128)(2,1)S(1)}, bf16[32,32,3,3]{1,0,3,2:T(8,128)(2,1)}, u32[]{:S(2)}) copy-start(bf16[32,32,3,3]{1,0,3,2:T(8,128)(2,1)} %param.16) | copy-start | bytes 55300
  1.5 73.6 %collective-permute-start.6 = (bf16[1,1,2048]{2,1,0:T(2,128)(2,1)S(1)}, bf16[1,1,2048]{2,1,0:T(2,128)(2,1)S(1)}, u32[]{:S(2)}, u32[]{:S(2)}) collective-permute-start(bf16[1,1,2048]{2,1,0:T(2,128)(2,1)S(1)} %get-tuple-element.165), channel_id=1, source_target_pairs={{0,1},{1,2},{2,3},{3,4},{4,5},{5,6},{6,7},{7,8},{8,9},{9,10},{10,1... | collective-permute-start | bytes 12296 | tf_op jit(solution)/shard_map/ppermute | solution.py:26
  3.9 71.3 %collective-permute-start.7 = (bf16[1,1,2048]{2,1,0:T(2,128)(2,1)S(1)}, bf16[1,1,2048]{2,1,0:T(2,128)(2,1)S(1)}, u32[]{:S(2)}, u32[]{:S(2)}) collective-permute-start(bf16[1,1,2048]{2,1,0:T(2,128)(2,1)S(1)} %get-tuple-element.166), channel_id=1, source_target_pairs={{1,0},{2,1},{3,2},{4,3},{5,4},{6,5},{7,6},{8,7},{9,8},{10,9},{11,1... | collective-permute-start | bytes 12296 | tf_op jit(solution)/shard_map/ppermute | solution.py:27
  8.6 73.6 %copy-start.17 = (f32[2048]{0:T(1024)}, f32[2048]{0:T(1024)S(1)}, u32[]{:S(2)}) copy-start(f32[2048]{0:T(1024)S(1)} %broadcast_bitcast_fusion.24) | copy-start | bytes 24580
  8.7 73.5 %copy-start.19 = (f32[2048]{0:T(1024)}, f32[2048]{0:T(1024)S(1)}, u32[]{:S(2)}) copy-start(f32[2048]{0:T(1024)S(1)} %get-tuple-element.216) | copy-start | bytes 24580
  8.7 73.5 %copy-start.21 = (f32[2048]{0:T(1024)}, f32[2048]{0:T(1024)S(1)}, u32[]{:S(2)}) copy-start(f32[2048]{0:T(1024)S(1)} %get-tuple-element.217) | copy-start | bytes 24580
  8.7 73.3 %copy-start.39 = (f32[2048]{0:T(1024)}, f32[2048]{0:T(1024)S(1)}, u32[]{:S(2)}) copy-start(f32[2048]{0:T(1024)S(1)} %get-tuple-element.194) | copy-start | bytes 24580
  8.7 73.3 %copy-start.41 = (f32[2048]{0:T(1024)}, f32[2048]{0:T(1024)S(1)}, u32[]{:S(2)}) copy-start(f32[2048]{0:T(1024)S(1)} %get-tuple-element.195) | copy-start | bytes 24580
  8.8 73.3 %copy-start.49 = (f32[2048]{0:T(1024)}, f32[2048]{0:T(1024)S(1)}, u32[]{:S(2)}) copy-start(f32[2048]{0:T(1024)S(1)} %get-tuple-element.197) | copy-start | bytes 24580
  9.2 73.3 %copy-start.23 = (f32[2048]{0:T(1024)}, f32[2048]{0:T(1024)S(1)}, u32[]{:S(2)}) copy-start(f32[2048]{0:T(1024)S(1)} %get-tuple-element.206) | copy-start | bytes 24580
  22.0 16.2 %all-to-all-start = ((f32[16,8,128]{2,1,0:T(8,128)}), f32[16,8,128]{2,1,0:T(8,128)S(1)}, u32[]{:S(2)}, u32[]{:S(2)}) async-start(f32[16,8,128]{2,1,0:T(8,128)} %constant_dynamic-update-slice_fusion), calls=%async_computation | async-start | bytes 131072 | tf_op jit(solution)/shard_map/all_to_all | solution.py:15
  71.1 11.0 %all-to-all-start.1 = ((f32[16,8,128]{2,1,0:T(8,128)}), f32[16,8,128]{2,1,0:T(8,128)S(1)}, u32[]{:S(2)}, u32[]{:S(2)}) async-start(f32[16,8,128]{2,1,0:T(8,128)} %fusion.342), calls=%async_computation.1 | async-start | bytes 131072 | tf_op jit(solution)/shard_map/all_to_all | solution.py:122
  83.7 18.0 %collective-permute-start = (bf16[1,1,2048]{2,1,0:T(2,128)(2,1)S(1)}, bf16[1,1,2048]{2,1,0:T(2,128)(2,1)S(1)}, u32[]{:S(2)}, u32[]{:S(2)}) collective-permute-start(bf16[1,1,2048]{2,1,0:T(2,128)(2,1)S(1)} %get-tuple-element.167), channel_id=1, source_target_pairs={{0,1},{1,2},{2,3},{3,4},{4,5},{5,6},{6,7},{7,8},{8,9},{9,10},{10,1... | collective-permute-start | bytes 12296 | tf_op jit(solution)/shard_map/ppermute | solution.py:26
  85.1 16.5 %collective-permute-start.1 = (bf16[1,1,2048]{2,1,0:T(2,128)(2,1)S(1)}, bf16[1,1,2048]{2,1,0:T(2,128)(2,1)S(1)}, u32[]{:S(2)}, u32[]{:S(2)}) collective-permute-start(bf16[1,1,2048]{2,1,0:T(2,128)(2,1)S(1)} %get-tuple-element.168), channel_id=1, source_target_pairs={{1,0},{2,1},{3,2},{4,3},{5,4},{6,5},{7,6},{8,7},{9,8},{10,9},{11,1... | collective-permute-start | bytes 12296 | tf_op jit(solution)/shard_map/ppermute | solution.py:27
  126.2 5.2 %collective-permute-start.2 = (bf16[32,1,2048]{2,0,1:T(8,128)(2,1)S(1)}, bf16[32,1,2048]{2,0,1:T(8,128)(2,1)S(1)}, u32[]{:S(2)}, u32[]{:S(2)}) collective-permute-start(bf16[32,1,2048]{2,0,1:T(8,128)(2,1)S(1)} %get-tuple-element.57), channel_id=1, source_target_pairs={{0,1},{1,2},{2,3},{3,4},{4,5},{5,6},{6,7},{7,8},{8,9},{9,10},{10,1... | collective-permute-start | bytes 393224 | tf_op jit(solution)/shard_map/ppermute | solution.py:26
  129.4 4.5 collective-permute-start.3
  204.9 18.9 %collective-permute-start.4 = (bf16[32,1,2048]{2,0,1:T(8,128)(2,1)}, bf16[32,1,2048]{2,0,1:T(8,128)(2,1)}, u32[]{:S(2)}, u32[]{:S(2)}) collective-permute-start(bf16[32,1,2048]{2,0,1:T(8,128)(2,1)} %get-tuple-element.55), channel_id=1, source_target_pairs={{0,1},{1,2},{2,3},{3,4},{4,5},{5,6},{6,7},{7,8},{8,9},{9,10},{10,1... | collective-permute-start | bytes 393224 | tf_op jit(solution)/shard_map/ppermute | solution.py:26
  211.0 12.8 %collective-permute-start.5 = (bf16[32,1,2048]{2,0,1:T(8,128)(2,1)}, bf16[32,1,2048]{2,0,1:T(8,128)(2,1)}, u32[]{:S(2)}, u32[]{:S(2)}) collective-permute-start(bf16[32,1,2048]{2,0,1:T(8,128)(2,1)} %get-tuple-element.56), channel_id=1, source_target_pairs={{1,0},{2,1},{3,2},{4,3},{5,4},{6,5},{7,6},{8,7},{9,8},{10,9},{11,1... | collective-permute-start | bytes 393224 | tf_op jit(solution)/shard_map/ppermute | solution.py:27
  212.3 7.0 %collective-permute-start.8 = (bf16[32,1,2048]{2,0,1:T(8,128)(2,1)}, bf16[32,1,2048]{2,0,1:T(8,128)(2,1)S(1)}, u32[]{:S(2)}, u32[]{:S(2)}) collective-permute-start(bf16[32,1,2048]{2,0,1:T(8,128)(2,1)} %get-tuple-element.53), channel_id=1, source_target_pairs={{0,1},{1,2},{2,3},{3,4},{4,5},{5,6},{6,7},{7,8},{8,9},{9,10},{10,1... | collective-permute-start | bytes 393224 | tf_op jit(solution)/shard_map/ppermute | solution.py:26
  215.4 5.0 %collective-permute-start.9 = (bf16[32,1,2048]{2,0,1:T(8,128)(2,1)S(1)}, bf16[32,1,2048]{2,0,1:T(8,128)(2,1)S(1)}, u32[]{:S(2)}, u32[]{:S(2)}) collective-permute-start(bf16[32,1,2048]{2,0,1:T(8,128)(2,1)S(1)} %get-tuple-element.54), channel_id=1, source_target_pairs={{1,0},{2,1},{3,2},{4,3},{5,4},{6,5},{7,6},{8,7},{9,8},{10,9},{11,1... | collective-permute-start | bytes 393224 | tf_op jit(solution)/shard_map/ppermute | solution.py:27
  306.7 7.9 %collective-permute-start.10 = (bf16[32,1,2048]{2,0,1:T(8,128)(2,1)S(1)}, bf16[32,1,2048]{2,0,1:T(8,128)(2,1)S(1)}, u32[]{:S(2)}, u32[]{:S(2)}) collective-permute-start(bf16[32,1,2048]{2,0,1:T(8,128)(2,1)S(1)} %get-tuple-element.51), channel_id=1, source_target_pairs={{0,1},{1,2},{2,3},{3,4},{4,5},{5,6},{6,7},{7,8},{8,9},{9,10},{10,1... | collective-permute-start | bytes 393224 | tf_op jit(solution)/shard_map/ppermute | solution.py:26
  312.2 3.2 collective-permute-start.11
  357.1 15.7 %all-to-all-start.2 = ((f32[16,8,128]{2,1,0:T(8,128)}), f32[16,8,128]{2,1,0:T(8,128)S(1)}, u32[]{:S(2)}, u32[]{:S(2)}) async-start(f32[16,8,128]{2,1,0:T(8,128)} %constant_dynamic-update-slice_fusion.16), calls=%async_computation.2 | async-start | bytes 131072 | tf_op jit(solution)/shard_map/all_to_all | solution.py:15
  404.9 67.7 %all-to-all-start.3 = ((f32[16,8,128]{2,1,0:T(8,128)}), f32[16,8,128]{2,1,0:T(8,128)S(1)}, u32[]{:S(2)}, u32[]{:S(2)}) async-start(f32[16,8,128]{2,1,0:T(8,128)} %fusion.341), calls=%async_computation.3 | async-start | bytes 131072 | tf_op jit(solution)/shard_map/all_to_all | solution.py:122
  (76 other events, 1563.8 us)
